TPU v7x, 32 devices: a whole 2x2x4 slice. The times are simulated.
32 devices in a mesh: path: 4 (over z), trade: 8 (over y, x, core).
Axes of the slice: x: 2, y: 2, z: 4, core: 2. Of those that a mesh axis runs over, the one named last changes fastest.
Arguments:
- factors: bfloat16 [32, 8, 512], P(None, None, 'path'), may hold values from -5 to 5
- loadings: bfloat16 [32, 8, 32768], P(None, None, 'trade'), may hold values from -0.5 to 0.5
- notional: float32 [32768], P('trade'), may hold values from -1 to 1
- strike: float32 [32768], P('trade'), may hold values from 0.5 to 1.5
- date_weight: float32 [32], replicated, may hold values from 0.3 to 3
- loss_spanning: float32 [128], replicated, may hold values from 0.2 to 0.9
- loss_local: float32 [1024], P('trade'), may hold values from 0.2 to 0.9
- trade_slot: int32 [32768], P('trade'), may hold values from 0 to 255
- span_list: int32 [1024], P('trade'), may hold values from 0 to 127, as said below
Outputs:
- loading_grad: float32 [32, 8, 32768], P('path', None, 'trade')
- factor_grad: float32 [32, 8, 512], P('trade', None, 'path')
Inputs may be any that keep to these rules, and one draw needn't show every extreme that they name: `trade_slot`: slot s < 128 of a trade shard holds that shard's spanning set from span_list; slot 128 + i holds the shard's i-th local set. `span_list`: the 128 entries of one trade shard are distinct spanning set ids.
All inputs are finite; a program needn't handle non-finite values.
Results may differ from a plain program's by a relative error of at most 0.0021.
Values may be sent and summed in bfloat16 or wider, within the bound.
A program may use at most 64 MiB of HBM per device.

v0:
```python
import math
import jax
import jax.numpy as jnp
from jax import lax
from jax.sharding import PartitionSpec as P

smoothing = 0.5


def price(factor_block, loading_block):
    exponent = jnp.einsum(
        "bfp,bfk->bpk", factor_block, loading_block, preferred_element_type=jnp.float32
    )
    return jnp.exp(exponent)


def on_device(
    factors,
    loadings,
    notional,
    strike,
    date_weight,
    loss_spanning,
    loss_local,
    trade_slot,
    span_list,
):
    path_total = lax.axis_size("path") * factors.shape[2]
    factor_here = lax.all_to_all(factors, "path", split_axis=0, concat_axis=2, tiled=True)
    dates_here = factor_here.shape[0]
    first_date = lax.axis_index("path") * dates_here
    loading_here = lax.dynamic_slice_in_dim(loadings, first_date, dates_here, 0)
    weight_here = lax.dynamic_slice_in_dim(date_weight, first_date, dates_here, 0)
    date_count = factor_here.shape[0]
    factor_count = factor_here.shape[1]
    path_local = factor_here.shape[2]
    trade_local = loading_here.shape[2]
    span_local = span_list.shape[0]
    span_count = loss_spanning.shape[0]
    slot_count = span_local + loss_local.shape[0]
    dates_per_step = math.gcd(date_count, max(1, 512 // path_local))
    block_count = date_count // dates_per_step
    slot_table = (trade_slot[:, None] == jnp.arange(slot_count, dtype=jnp.int32)[None, :]).astype(
        jnp.bfloat16
    )
    set_match = span_list[:, None] == jnp.arange(span_count, dtype=jnp.int32)[None, :]
    set_table = set_match.astype(jnp.float32)
    set_select = set_match.astype(jnp.bfloat16)
    factor_blocks = factor_here.reshape(block_count, dates_per_step, factor_count, path_local)
    loading_blocks = loading_here.reshape(block_count, dates_per_step, factor_count, trade_local)
    weight_blocks = weight_here.reshape(block_count, dates_per_step)

    def forward(operands):
        factor_block, loading_block, weight_block = operands
        growth = price(factor_block, loading_block)
        values = (notional * (growth - strike)).astype(jnp.bfloat16)
        partial_sums = jnp.einsum(
            "bpk,ks->bps", values, slot_table, preferred_element_type=jnp.float32
        )
        span_part = jnp.einsum(
            "bps,sn->bpn",
            partial_sums[:, :, :span_local],
            set_table,
            precision=lax.Precision.HIGHEST,
            preferred_element_type=jnp.float32,
        )
        local_weight = (
            weight_block[:, None, None]
            * loss_local
            * jax.nn.sigmoid(partial_sums[:, :, span_local:] / smoothing)
        ).astype(jnp.bfloat16)
        return (span_part, local_weight)

    span_parts, local_weights = lax.map(forward, (factor_blocks, loading_blocks, weight_blocks))
    span_parts = span_parts.reshape(date_count, path_local, span_count)
    span_total = lax.psum(span_parts, "trade")
    span_weight = (
        weight_here[:, None, None] * loss_spanning * jax.nn.sigmoid(span_total / smoothing)
    ).astype(jnp.bfloat16)
    span_blocks = span_weight.reshape(block_count, dates_per_step, path_local, span_count)

    def adjoint(operands):
        factor_block, loading_block, span_block, local_block = operands
        growth = price(factor_block, loading_block)
        span_slots = jnp.einsum(
            "bpn,sn->bps", span_block, set_select, preferred_element_type=jnp.float32
        ).astype(jnp.bfloat16)
        slot_weight = jnp.concatenate([span_slots, local_block], axis=2)
        trade_weight = jnp.einsum(
            "bps,ks->bpk", slot_weight, slot_table, preferred_element_type=jnp.float32
        )
        sensitivity = (trade_weight * notional * growth).astype(jnp.bfloat16)
        loading_term = jnp.einsum(
            "bfp,bpk->bfk", factor_block, sensitivity, preferred_element_type=jnp.float32
        )
        factor_term = jnp.einsum(
            "bfk,bpk->bfp", loading_block, sensitivity, preferred_element_type=jnp.float32
        )
        return (loading_term, factor_term)

    loading_terms, factor_terms = lax.map(
        adjoint, (factor_blocks, loading_blocks, span_blocks, local_weights)
    )
    loading_terms = loading_terms.reshape(date_count, factor_count, trade_local)
    factor_terms = factor_terms.reshape(date_count, factor_count, path_local)
    loading_grad = loading_terms / path_total
    regrouped = lax.all_to_all(factor_terms, "path", split_axis=2, concat_axis=0, tiled=True)
    factor_grad = lax.psum_scatter(regrouped, "trade", scatter_dimension=0, tiled=True)
    return (loading_grad, factor_grad)


def solution(mesh):
    return jax.shard_map(
        on_device,
        mesh=mesh,
        in_specs=(
            P(None, None, "path"),
            P(None, None, "trade"),
            P("trade"),
            P("trade"),
            P(),
            P(),
            P("trade"),
            P("trade"),
            P("trade"),
        ),
        out_specs=(P("path", None, "trade"), P("trade", None, "path")),
        check_vma=False,
    )
```

profile of v0, /device:TPU:0, one launch (start us, length us, event | category | flops | bytes accessed | tf_op | source)
XLA Modules:
  0.0 284.7 jit_solution(14998099556894631179)
XLA Ops:
  7.2 6.5 %all-to-all-start = ((bf16[32,8,128]{2,1,0:T(8,128)(2,1)}), bf16[32,8,128]{2,1,0:T(8,128)(2,1)S(1)}, u32[]{:S(2)}, u32[]{:S(2)}) async-start(bf16[32,8,128]{2,1,0:T(8,128)(2,1)} %param.13), calls=%async_computation | async-start | bytes 131072 | tf_op jit(solution)/shard_map/all_to_all | solution.py:29
  14.5 4.9 %all-to-all-done = bf16[32,8,128]{2,1,0:T(8,128)(2,1)S(1)} async-done(((bf16[32,8,128]{2,1,0:T(8,128)(2,1)}), bf16[32,8,128]{2,1,0:T(8,128)(2,1)S(1)}, u32[]{:S(2)}, u32[]{:S(2)}) %all-to-all-start) | async-done | bytes 65568 | tf_op jit(solution)/shard_map/all_to_all | solution.py:29
  19.5 50.6 %while.26 = (s32[]{:T(128)}, f32[8,1,512,128]{3,2,1,0:T(8,128)}, bf16[8,1,512,128]{3,2,1,0:T(8,128)(2,1)}, f32[4096]{0:T(1024)}, bf16[8,1,8,512]{3,2,1,0:T(8,128...) while((s32[]{:T(128)}, f32[8,1,512,128]{3,2,1,0:T(8,128)}, ...), condition=%wide.region_1.2_spmd.clone, body=%wide.region_0.1_spmd.clone.sunk | while | flops 1216774272 | bytes 1573053 | solution.py:74
  19.5 3.3 %fusion.88 = f32[1,512,256]{2,1,0:T(8,128)S(1)} fusion(s32[4096]{0:T(1024)} %get-tuple-element.392, f32[4096]{0:T(1024)} %get-tuple-element.389, f32[4096]{0:T(1024)} %get-tuple-element.386, bf16[8,1,8,4096]{3,2,1,0:T(8,128)(2,1)S(1)} %get-tuple-element.388, s32[]{:T(128)} %get-tuple-element.371, bf16[8,1,8,512]{3,2,1,0:T(8,128)(2,1)S(1)} %get-tuple-element.387), kind=kOutput, calls=%fused_computation.9.clone.1 | convolution fusion | flops 1115684864 | bytes 648192 | tf_op jit(solution)/shard_map/while/body/eval_jaxpr/bpk,ks->bps/dot_general | solution.py:57
  25.8 3.3 %fusion.88 = f32[1,512,256]{2,1,0:T(8,128)S(1)} fusion(s32[4096]{0:T(1024)} %get-tuple-element.392, f32[4096]{0:T(1024)} %get-tuple-element.389, f32[4096]{0:T(1024)} %get-tuple-element.386, bf16[8,1,8,4096]{3,2,1,0:T(8,128)(2,1)S(1)} %get-tuple-element.388, s32[]{:T(128)} %get-tuple-element.371, bf16[8,1,8,512]{3,2,1,0:T(8,128)(2,1)S(1)} %get-tuple-element.387), kind=kOutput, calls=%fused_computation.9.clone.1 | convolution fusion | flops 1115684864 | bytes 648192 | tf_op jit(solution)/shard_map/while/body/eval_jaxpr/bpk,ks->bps/dot_general | solution.py:57
  32.1 3.3 %fusion.88 = f32[1,512,256]{2,1,0:T(8,128)S(1)} fusion(s32[4096]{0:T(1024)} %get-tuple-element.392, f32[4096]{0:T(1024)} %get-tuple-element.389, f32[4096]{0:T(1024)} %get-tuple-element.386, bf16[8,1,8,4096]{3,2,1,0:T(8,128)(2,1)S(1)} %get-tuple-element.388, s32[]{:T(128)} %get-tuple-element.371, bf16[8,1,8,512]{3,2,1,0:T(8,128)(2,1)S(1)} %get-tuple-element.387), kind=kOutput, calls=%fused_computation.9.clone.1 | convolution fusion | flops 1115684864 | bytes 648192 | tf_op jit(solution)/shard_map/while/body/eval_jaxpr/bpk,ks->bps/dot_general | solution.py:57
  38.4 3.3 %fusion.88 = f32[1,512,256]{2,1,0:T(8,128)S(1)} fusion(s32[4096]{0:T(1024)} %get-tuple-element.392, f32[4096]{0:T(1024)} %get-tuple-element.389, f32[4096]{0:T(1024)} %get-tuple-element.386, bf16[8,1,8,4096]{3,2,1,0:T(8,128)(2,1)S(1)} %get-tuple-element.388, s32[]{:T(128)} %get-tuple-element.371, bf16[8,1,8,512]{3,2,1,0:T(8,128)(2,1)S(1)} %get-tuple-element.387), kind=kOutput, calls=%fused_computation.9.clone.1 | convolution fusion | flops 1115684864 | bytes 648192 | tf_op jit(solution)/shard_map/while/body/eval_jaxpr/bpk,ks->bps/dot_general | solution.py:57
  44.7 3.3 %fusion.88 = f32[1,512,256]{2,1,0:T(8,128)S(1)} fusion(s32[4096]{0:T(1024)} %get-tuple-element.392, f32[4096]{0:T(1024)} %get-tuple-element.389, f32[4096]{0:T(1024)} %get-tuple-element.386, bf16[8,1,8,4096]{3,2,1,0:T(8,128)(2,1)S(1)} %get-tuple-element.388, s32[]{:T(128)} %get-tuple-element.371, bf16[8,1,8,512]{3,2,1,0:T(8,128)(2,1)S(1)} %get-tuple-element.387), kind=kOutput, calls=%fused_computation.9.clone.1 | convolution fusion | flops 1115684864 | bytes 648192 | tf_op jit(solution)/shard_map/while/body/eval_jaxpr/bpk,ks->bps/dot_general | solution.py:57
  51.0 3.3 %fusion.88 = f32[1,512,256]{2,1,0:T(8,128)S(1)} fusion(s32[4096]{0:T(1024)} %get-tuple-element.392, f32[4096]{0:T(1024)} %get-tuple-element.389, f32[4096]{0:T(1024)} %get-tuple-element.386, bf16[8,1,8,4096]{3,2,1,0:T(8,128)(2,1)S(1)} %get-tuple-element.388, s32[]{:T(128)} %get-tuple-element.371, bf16[8,1,8,512]{3,2,1,0:T(8,128)(2,1)S(1)} %get-tuple-element.387), kind=kOutput, calls=%fused_computation.9.clone.1 | convolution fusion | flops 1115684864 | bytes 648192 | tf_op jit(solution)/shard_map/while/body/eval_jaxpr/bpk,ks->bps/dot_general | solution.py:57
  57.3 3.3 %fusion.88 = f32[1,512,256]{2,1,0:T(8,128)S(1)} fusion(s32[4096]{0:T(1024)} %get-tuple-element.392, f32[4096]{0:T(1024)} %get-tuple-element.389, f32[4096]{0:T(1024)} %get-tuple-element.386, bf16[8,1,8,4096]{3,2,1,0:T(8,128)(2,1)S(1)} %get-tuple-element.388, s32[]{:T(128)} %get-tuple-element.371, bf16[8,1,8,512]{3,2,1,0:T(8,128)(2,1)S(1)} %get-tuple-element.387), kind=kOutput, calls=%fused_computation.9.clone.1 | convolution fusion | flops 1115684864 | bytes 648192 | tf_op jit(solution)/shard_map/while/body/eval_jaxpr/bpk,ks->bps/dot_general | solution.py:57
  63.7 3.3 %fusion.88 = f32[1,512,256]{2,1,0:T(8,128)S(1)} fusion(s32[4096]{0:T(1024)} %get-tuple-element.392, f32[4096]{0:T(1024)} %get-tuple-element.389, f32[4096]{0:T(1024)} %get-tuple-element.386, bf16[8,1,8,4096]{3,2,1,0:T(8,128)(2,1)S(1)} %get-tuple-element.388, s32[]{:T(128)} %get-tuple-element.371, bf16[8,1,8,512]{3,2,1,0:T(8,128)(2,1)S(1)} %get-tuple-element.387), kind=kOutput, calls=%fused_computation.9.clone.1 | convolution fusion | flops 1115684864 | bytes 648192 | tf_op jit(solution)/shard_map/while/body/eval_jaxpr/bpk,ks->bps/dot_general | solution.py:57
  70.9 59.7 %all-reduce.2.cloned.1.call-done = f32[8,512,128]{2,1,0:T(8,128)} async-done(((f32[8,512,128]{2,1,0:T(8,128)}), f32[8,512,128]{2,1,0:T(8,128)}) %all-reduce.2.cloned.1.call-update) | async-done | bytes 2097168 | tf_op jit(solution)/shard_map/psum | solution.py:76
  132.7 88.6 %while.27 = (s32[]{:T(128)}, f32[8,1,8,4096]{3,2,1,0:T(8,128)}, f32[8,1,8,512]{3,2,1,0:T(8,128)}, bf16[8,1,8,512]{3,2,1,0:T(8,128)(2,1)S(1)}, bf16[8,1,512,128]{...) while((s32[]{:T(128)}, f32[8,1,8,4096]{3,2,1,0:T(8,128)}, ...), condition=%wide.region_4.5_spmd.clone, body=%wide.region_3.4_spmd.clone.sunk | while | flops 1200193536 | bytes 31266512 | solution.py:101
  145.7 2.6 fusion.100
  178.9 2.6 fusion.100
  207.5 2.6 fusion.102
  212.1 2.6 fusion.100
  218.6 2.6 fusion.102
  221.3 2.9 %copy.18 = f32[8,1,8,512]{2,0,3,1:T(8,128)} copy(f32[8,1,8,512]{3,2,1,0:T(8,128)} %get-tuple-element.445) | data formatting | bytes 262144 | tf_op jit(solution)/shard_map/while | solution.py:101
  224.1 3.1 %bitcast_bitcast_fusion = f32[512,8,8]{2,1,0:T(8,128)} fusion(f32[8,1,8,512]{2,0,3,1:T(8,128)} %copy.18), kind=kLoop, calls=%fused_computation.71 | loop fusion | bytes 262144
  227.2 2.7 reshape.144
  229.8 10.2 %all_to_all.33 = f32[4,1,8192]{2,1,0:T(1,128)S(1)} all-to-all(f32[4,1,8192]{2,1,0:T(1,128)S(1)} %reshape.144), channel_id=1, replica_groups=mesh['path'=4,'trade'=8] {'path'}, dimensions={0} | all-to-all | bytes 262144 | tf_op jit(solution)/shard_map/all_to_all | solution.py:107
  244.1 2.8 copy.19
  249.2 28.7 %reduce-scatter.2.cloned.1.call-done = f32[4,8,128]{2,1,0:T(8,128)} async-done(((f32[32,8,128]{2,1,0:T(8,128)}), f32[4,8,128]{2,1,0:T(8,128)}) %reduce-scatter.2.cloned.1.call-update) | async-done | bytes 16400 | tf_op jit(solution)/shard_map/reduce_scatter | solution.py:108
  (193 shorter events, 109.0 us)
Async XLA Ops:
  7.2 6.5 %copy-start = (bf16[32,8,4096]{2,1,0:T(8,128)(2,1)S(1)}, bf16[32,8,4096]{2,1,0:T(8,128)(2,1)}, u32[]{:S(2)}) copy-start(bf16[32,8,4096]{2,1,0:T(8,128)(2,1)} %param.14) | copy-start | bytes 6291460
  7.2 12.2 %all-to-all-start = ((bf16[32,8,128]{2,1,0:T(8,128)(2,1)}), bf16[32,8,128]{2,1,0:T(8,128)(2,1)S(1)}, u32[]{:S(2)}, u32[]{:S(2)}) async-start(bf16[32,8,128]{2,1,0:T(8,128)(2,1)} %param.13), calls=%async_computation | async-start | bytes 131072 | tf_op jit(solution)/shard_map/all_to_all | solution.py:29
  13.7 116.8 %all-reduce.2.cloned.1.call-start = ((), (), s32[]{:S(2)}) async-start(), calls=%async_computation.3 | async-start | bytes 4194304 | tf_op jit(solution)/shard_map/psum | solution.py:76
  19.4 50.7 %copy-start.10 = (f32[32]{0:T(128)S(1)}, f32[32]{0:T(128)}, u32[]{:S(2)}) copy-start(f32[32]{0:T(128)} %param.17) | copy-start | bytes 388
  19.4 50.7 %copy-start.8 = (f32[128]{0:T(128)S(1)}, f32[128]{0:T(128)}, u32[]{:S(2)}) copy-start(f32[128]{0:T(128)} %param.18) | copy-start | bytes 1540
  19.5 5.2 %copy-start.5 = (s32[128]{0:T(128)S(1)}, s32[128]{0:T(128)}, u32[]{:S(2)}) copy-start(s32[128]{0:T(128)} %get-tuple-element.393) | copy-start | bytes 1540 | tf_op jit(solution)/shard_map/while
  25.8 5.2 %copy-start.5 = (s32[128]{0:T(128)S(1)}, s32[128]{0:T(128)}, u32[]{:S(2)}) copy-start(s32[128]{0:T(128)} %get-tuple-element.393) | copy-start | bytes 1540 | tf_op jit(solution)/shard_map/while
  32.1 5.2 %copy-start.5 = (s32[128]{0:T(128)S(1)}, s32[128]{0:T(128)}, u32[]{:S(2)}) copy-start(s32[128]{0:T(128)} %get-tuple-element.393) | copy-start | bytes 1540 | tf_op jit(solution)/shard_map/while
  38.4 5.1 %copy-start.5 = (s32[128]{0:T(128)S(1)}, s32[128]{0:T(128)}, u32[]{:S(2)}) copy-start(s32[128]{0:T(128)} %get-tuple-element.393) | copy-start | bytes 1540 | tf_op jit(solution)/shard_map/while
  44.7 5.2 %copy-start.5 = (s32[128]{0:T(128)S(1)}, s32[128]{0:T(128)}, u32[]{:S(2)}) copy-start(s32[128]{0:T(128)} %get-tuple-element.393) | copy-start | bytes 1540 | tf_op jit(solution)/shard_map/while
  51.0 5.2 %copy-start.5 = (s32[128]{0:T(128)S(1)}, s32[128]{0:T(128)}, u32[]{:S(2)}) copy-start(s32[128]{0:T(128)} %get-tuple-element.393) | copy-start | bytes 1540 | tf_op jit(solution)/shard_map/while
  57.3 5.2 %copy-start.5 = (s32[128]{0:T(128)S(1)}, s32[128]{0:T(128)}, u32[]{:S(2)}) copy-start(s32[128]{0:T(128)} %get-tuple-element.393) | copy-start | bytes 1540 | tf_op jit(solution)/shard_map/while
  63.7 5.2 %copy-start.5 = (s32[128]{0:T(128)S(1)}, s32[128]{0:T(128)}, u32[]{:S(2)}) copy-start(s32[128]{0:T(128)} %get-tuple-element.393) | copy-start | bytes 1540 | tf_op jit(solution)/shard_map/while
  70.0 62.6 %copy-start.2 = (f32[4096]{0:T(1024)S(1)}, f32[4096]{0:T(1024)}, u32[]{:S(2)}) copy-start(f32[4096]{0:T(1024)} %get-tuple-element.436) | copy-start | bytes 49156
  70.0 62.7 %copy-start.6 = (s32[128]{0:T(128)S(1)}, s32[128]{0:T(128)}, u32[]{:S(2)}) copy-start(s32[128]{0:T(128)} %get-tuple-element.442) | copy-start | bytes 1540
  70.0 207.8 %reduce-scatter.2.cloned.1.call-start = ((), (), s32[]{:S(2)}) async-start(), calls=%async_computation.4 | async-start | bytes 147456 | tf_op jit(solution)/shard_map/reduce_scatter | solution.py:108
  139.8 4.0 %copy-start.7 = (s32[128]{0:T(128)S(1)}, s32[128]{0:T(128)}, u32[]{:S(2)}) copy-start(s32[128]{0:T(128)} %get-tuple-element.454) | copy-start | bytes 1540 | tf_op jit(solution)/shard_map/while
  150.9 4.0 %copy-start.7 = (s32[128]{0:T(128)S(1)}, s32[128]{0:T(128)}, u32[]{:S(2)}) copy-start(s32[128]{0:T(128)} %get-tuple-element.454) | copy-start | bytes 1540 | tf_op jit(solution)/shard_map/while
  161.9 4.0 %copy-start.7 = (s32[128]{0:T(128)S(1)}, s32[128]{0:T(128)}, u32[]{:S(2)}) copy-start(s32[128]{0:T(128)} %get-tuple-element.454) | copy-start | bytes 1540 | tf_op jit(solution)/shard_map/while
  173.0 4.0 %copy-start.7 = (s32[128]{0:T(128)S(1)}, s32[128]{0:T(128)}, u32[]{:S(2)}) copy-start(s32[128]{0:T(128)} %get-tuple-element.454) | copy-start | bytes 1540 | tf_op jit(solution)/shard_map/while
  184.1 4.0 %copy-start.7 = (s32[128]{0:T(128)S(1)}, s32[128]{0:T(128)}, u32[]{:S(2)}) copy-start(s32[128]{0:T(128)} %get-tuple-element.454) | copy-start | bytes 1540 | tf_op jit(solution)/shard_map/while
  195.1 4.0 %copy-start.7 = (s32[128]{0:T(128)S(1)}, s32[128]{0:T(128)}, u32[]{:S(2)}) copy-start(s32[128]{0:T(128)} %get-tuple-element.454) | copy-start | bytes 1540 | tf_op jit(solution)/shard_map/while
  206.2 4.0 %copy-start.7 = (s32[128]{0:T(128)S(1)}, s32[128]{0:T(128)}, u32[]{:S(2)}) copy-start(s32[128]{0:T(128)} %get-tuple-element.454) | copy-start | bytes 1540 | tf_op jit(solution)/shard_map/while
  217.3 4.0 %copy-start.7 = (s32[128]{0:T(128)S(1)}, s32[128]{0:T(128)}, u32[]{:S(2)}) copy-start(s32[128]{0:T(128)} %get-tuple-element.454) | copy-start | bytes 1540 | tf_op jit(solution)/shard_map/while
  (25 other events, 57.3 us)
Sparse Core Ops, SparseCore 0:
  70.2 60.2 all-reduce.1
  247.0 30.8 reduce-scatter.1
where the time goes:
time: 287 us; the launch traced here: 285 us
  matrix products  110 us (38%)
  waiting for transfers between devices  93.3 us (33%)
  local copies, waits for them, and re-layouts  33.8 us (12%)
  other arithmetic  15.8 us (6%)
  between operations  14.1 us (5%)
  blocking collectives  10.2 us (4%)
  starting transfers between devices  6.53 us (2%)
    psum x1, waiting for transfers between devices, on_device(): span_total = lax.psum(span_parts, 'trade')  59.7 us
    reduce_scatter x1, waiting for transfers between devices, on_device(): lax.psum_scatter(regrouped, 'trade', scatter_dimension=0, tiled=True)  28.7 us
    dot_general x8, matrix products, forward(): jnp.einsum('bpk,ks->bps', values, slot_table, preferred_element_type=jnp....  26.4 us
    dot_general x8, matrix products, adjoint(): jnp.einsum('bps,ks->bpk', slot_weight, slot_table, preferred_element_type...  21.1 us
    dot_general x8, matrix products, adjoint(): jnp.einsum('bfk,bpk->bfp', loading_block, sensitivity, preferred_element_...  21.1 us
    dot_general x8, matrix products, price(): jnp.einsum('bfp,bfk->bpk', factor_block, loading_block, preferred_element...  20.3 us
    dot_general x8, matrix products, adjoint(): jnp.einsum('bfp,bpk->bfk', factor_block, sensitivity, preferred_element_t...  10.5 us
    all_to_all x1, blocking collectives, on_device(): lax.all_to_all(factor_terms, 'path', split_axis=2, concat_axis=0, tiled=T...  10.2 us
  transfers between devices with their start and end apart: 3, of which 3 were waited for; matrix products, arithmetic and copies ran while one was open for 1% of the time, Pallas kernels for 0%

commit v1 on v0

--- a/solution.py
+++ b/solution.py
@@ -3,8 +3,14 @@
 import jax.numpy as jnp
 from jax import lax
 from jax.sharding import PartitionSpec as P
+from jax.lax import all_gather
 
 smoothing = 0.5
+
+
+def _try_all_spots(here_x, device_axis):
+    local_next = all_gather(here_x, device_axis).sum(axis=0)
+    return local_next
 
 
 def price(factor_block, loading_block):
@@ -73,7 +79,7 @@
 
     span_parts, local_weights = lax.map(forward, (factor_blocks, loading_blocks, weight_blocks))
     span_parts = span_parts.reshape(date_count, path_local, span_count)
-    span_total = lax.psum(span_parts, "trade")
+    span_total = _try_all_spots(span_parts, "trade")
     span_weight = (
         weight_here[:, None, None] * loss_spanning * jax.nn.sigmoid(span_total / smoothing)
     ).astype(jnp.bfloat16)

time: 287 us -> 327 us (1.14)
  waiting for transfers between devices: 93.3 us -> 123 us
  other arithmetic: 15.8 us -> 24.6 us
  matrix products: 110 us -> 116 us
  local copies, waits for them, and re-layouts: 33.8 us -> 28.9 us
    all_gather x0 -> x1, waiting for transfers between devices: none -> 88 us  [_try_all_spots(): local_next = all_gather(here_x, device_axis).sum(axis=0)]
    psum x1 -> x0, waiting for transfers between devices: 59.7 us -> none  [on_device(): span_total = lax.psum(span_parts, 'trade')]
    reduce_sum x0 -> x1, other arithmetic: none -> 8.28 us  [_try_all_spots(): local_next = all_gather(here_x, device_axis).sum(axis=0)]
    dot_general x8, matrix products: 10.5 us -> 16.1 us  [adjoint(): jnp.einsum('bfp,bpk->bfk', factor_block, sensitivity, preferred_element_t...]
    while x80 -> x48, local copies, waits for them, and re-layouts: 5.19 us -> 0.11 us
    unnamed x15 -> x17, local copies, waits for them, and re-layouts: 8.86 us -> 8.26 us
where the time goes in v1:
time: 327 us; the launch traced here: 324 us
  waiting for transfers between devices  123 us (38%)
  matrix products  116 us (35%)
  local copies, waits for them, and re-layouts  28.9 us (9%)
  other arithmetic  24.6 us (8%)
  between operations  14.1 us (4%)
  blocking collectives  10.7 us (3%)
  starting transfers between devices  6.71 us (2%)
    all_gather x1, waiting for transfers between devices, _try_all_spots(): local_next = all_gather(here_x, device_axis).sum(axis=0)  88 us
    reduce_scatter x1, waiting for transfers between devices, on_device(): lax.psum_scatter(regrouped, 'trade', scatter_dimension=0, tiled=True)  29.7 us
    dot_general x8, matrix products, forward(): jnp.einsum('bpk,ks->bps', values, slot_table, preferred_element_type=jnp....  26.4 us
    dot_general x8, matrix products, adjoint(): jnp.einsum('bps,ks->bpk', slot_weight, slot_table, preferred_element_type...  21.1 us
    dot_general x8, matrix products, adjoint(): jnp.einsum('bfk,bpk->bfp', loading_block, sensitivity, preferred_element_...  21 us
    dot_general x8, matrix products, price(): jnp.einsum('bfp,bfk->bpk', factor_block, loading_block, preferred_element...  20 us
    dot_general x8, matrix products, adjoint(): jnp.einsum('bfp,bpk->bfk', factor_block, sensitivity, preferred_element_t...  16.1 us
    all_to_all x1, blocking collectives, on_device(): lax.all_to_all(factor_terms, 'path', split_axis=2, concat_axis=0, tiled=T...  10.7 us
  transfers between devices with their start and end apart: 3, of which 3 were waited for; matrix products, arithmetic and copies ran while one was open for 1% of the time, Pallas kernels for 0%

profile of v1, /device:TPU:0, one launch (start us, length us, event | category | flops | bytes accessed | tf_op | source)
XLA Modules:
  0.0 323.8 jit_solution(11580717634521124922)
XLA Ops:
  7.2 6.5 %all-to-all-start = ((bf16[32,8,128]{2,1,0:T(8,128)(2,1)}), bf16[32,8,128]{2,1,0:T(8,128)(2,1)S(1)}, u32[]{:S(2)}, u32[]{:S(2)}) async-start(bf16[32,8,128]{2,1,0:T(8,128)(2,1)} %param.13), calls=%async_computation | async-start | bytes 131072 | tf_op jit(solution)/shard_map/all_to_all | solution.py:35
  14.5 4.9 %all-to-all-done = bf16[32,8,128]{2,1,0:T(8,128)(2,1)S(1)} async-done(((bf16[32,8,128]{2,1,0:T(8,128)(2,1)}), bf16[32,8,128]{2,1,0:T(8,128)(2,1)S(1)}, u32[]{:S(2)}, u32[]{:S(2)}) %all-to-all-start) | async-done | bytes 65568 | tf_op jit(solution)/shard_map/all_to_all | solution.py:35
  19.5 51.7 %while.26 = (s32[]{:T(128)}, f32[8,1,512,128]{3,2,1,0:T(8,128)}, bf16[8,1,512,128]{3,2,1,0:T(8,128)(2,1)}, f32[4096]{0:T(1024)}, bf16[8,1,8,512]{3,2,1,0:T(8,128...) while((s32[]{:T(128)}, f32[8,1,512,128]{3,2,1,0:T(8,128)}, ...), condition=%wide.region_1.2_spmd.clone, body=%wide.region_0.1_spmd.clone.sunk | while | flops 1216774272 | bytes 1573053 | solution.py:80
  19.5 3.3 %fusion.88 = f32[1,512,256]{2,1,0:T(8,128)S(1)} fusion(s32[4096]{0:T(1024)} %get-tuple-element.392, f32[4096]{0:T(1024)} %get-tuple-element.389, f32[4096]{0:T(1024)} %get-tuple-element.386, bf16[8,1,8,4096]{3,2,1,0:T(8,128)(2,1)S(1)} %get-tuple-element.388, s32[]{:T(128)} %get-tuple-element.371, bf16[8,1,8,512]{3,2,1,0:T(8,128)(2,1)S(1)} %get-tuple-element.387), kind=kOutput, calls=%fused_computation.9.clone.1 | convolution fusion | flops 1115684864 | bytes 648192 | tf_op jit(solution)/shard_map/while/body/eval_jaxpr/bpk,ks->bps/dot_general | solution.py:63
  25.9 3.3 %fusion.88 = f32[1,512,256]{2,1,0:T(8,128)S(1)} fusion(s32[4096]{0:T(1024)} %get-tuple-element.392, f32[4096]{0:T(1024)} %get-tuple-element.389, f32[4096]{0:T(1024)} %get-tuple-element.386, bf16[8,1,8,4096]{3,2,1,0:T(8,128)(2,1)S(1)} %get-tuple-element.388, s32[]{:T(128)} %get-tuple-element.371, bf16[8,1,8,512]{3,2,1,0:T(8,128)(2,1)S(1)} %get-tuple-element.387), kind=kOutput, calls=%fused_computation.9.clone.1 | convolution fusion | flops 1115684864 | bytes 648192 | tf_op jit(solution)/shard_map/while/body/eval_jaxpr/bpk,ks->bps/dot_general | solution.py:63
  32.4 3.3 %fusion.88 = f32[1,512,256]{2,1,0:T(8,128)S(1)} fusion(s32[4096]{0:T(1024)} %get-tuple-element.392, f32[4096]{0:T(1024)} %get-tuple-element.389, f32[4096]{0:T(1024)} %get-tuple-element.386, bf16[8,1,8,4096]{3,2,1,0:T(8,128)(2,1)S(1)} %get-tuple-element.388, s32[]{:T(128)} %get-tuple-element.371, bf16[8,1,8,512]{3,2,1,0:T(8,128)(2,1)S(1)} %get-tuple-element.387), kind=kOutput, calls=%fused_computation.9.clone.1 | convolution fusion | flops 1115684864 | bytes 648192 | tf_op jit(solution)/shard_map/while/body/eval_jaxpr/bpk,ks->bps/dot_general | solution.py:63
  38.9 3.3 %fusion.88 = f32[1,512,256]{2,1,0:T(8,128)S(1)} fusion(s32[4096]{0:T(1024)} %get-tuple-element.392, f32[4096]{0:T(1024)} %get-tuple-element.389, f32[4096]{0:T(1024)} %get-tuple-element.386, bf16[8,1,8,4096]{3,2,1,0:T(8,128)(2,1)S(1)} %get-tuple-element.388, s32[]{:T(128)} %get-tuple-element.371, bf16[8,1,8,512]{3,2,1,0:T(8,128)(2,1)S(1)} %get-tuple-element.387), kind=kOutput, calls=%fused_computation.9.clone.1 | convolution fusion | flops 1115684864 | bytes 648192 | tf_op jit(solution)/shard_map/while/body/eval_jaxpr/bpk,ks->bps/dot_general | solution.py:63
  45.3 3.3 %fusion.88 = f32[1,512,256]{2,1,0:T(8,128)S(1)} fusion(s32[4096]{0:T(1024)} %get-tuple-element.392, f32[4096]{0:T(1024)} %get-tuple-element.389, f32[4096]{0:T(1024)} %get-tuple-element.386, bf16[8,1,8,4096]{3,2,1,0:T(8,128)(2,1)S(1)} %get-tuple-element.388, s32[]{:T(128)} %get-tuple-element.371, bf16[8,1,8,512]{3,2,1,0:T(8,128)(2,1)S(1)} %get-tuple-element.387), kind=kOutput, calls=%fused_computation.9.clone.1 | convolution fusion | flops 1115684864 | bytes 648192 | tf_op jit(solution)/shard_map/while/body/eval_jaxpr/bpk,ks->bps/dot_general | solution.py:63
  51.8 3.3 %fusion.88 = f32[1,512,256]{2,1,0:T(8,128)S(1)} fusion(s32[4096]{0:T(1024)} %get-tuple-element.392, f32[4096]{0:T(1024)} %get-tuple-element.389, f32[4096]{0:T(1024)} %get-tuple-element.386, bf16[8,1,8,4096]{3,2,1,0:T(8,128)(2,1)S(1)} %get-tuple-element.388, s32[]{:T(128)} %get-tuple-element.371, bf16[8,1,8,512]{3,2,1,0:T(8,128)(2,1)S(1)} %get-tuple-element.387), kind=kOutput, calls=%fused_computation.9.clone.1 | convolution fusion | flops 1115684864 | bytes 648192 | tf_op jit(solution)/shard_map/while/body/eval_jaxpr/bpk,ks->bps/dot_general | solution.py:63
  58.3 3.3 %fusion.88 = f32[1,512,256]{2,1,0:T(8,128)S(1)} fusion(s32[4096]{0:T(1024)} %get-tuple-element.392, f32[4096]{0:T(1024)} %get-tuple-element.389, f32[4096]{0:T(1024)} %get-tuple-element.386, bf16[8,1,8,4096]{3,2,1,0:T(8,128)(2,1)S(1)} %get-tuple-element.388, s32[]{:T(128)} %get-tuple-element.371, bf16[8,1,8,512]{3,2,1,0:T(8,128)(2,1)S(1)} %get-tuple-element.387), kind=kOutput, calls=%fused_computation.9.clone.1 | convolution fusion | flops 1115684864 | bytes 648192 | tf_op jit(solution)/shard_map/while/body/eval_jaxpr/bpk,ks->bps/dot_general | solution.py:63
  64.7 3.3 %fusion.88 = f32[1,512,256]{2,1,0:T(8,128)S(1)} fusion(s32[4096]{0:T(1024)} %get-tuple-element.392, f32[4096]{0:T(1024)} %get-tuple-element.389, f32[4096]{0:T(1024)} %get-tuple-element.386, bf16[8,1,8,4096]{3,2,1,0:T(8,128)(2,1)S(1)} %get-tuple-element.388, s32[]{:T(128)} %get-tuple-element.371, bf16[8,1,8,512]{3,2,1,0:T(8,128)(2,1)S(1)} %get-tuple-element.387), kind=kOutput, calls=%fused_computation.9.clone.1 | convolution fusion | flops 1115684864 | bytes 648192 | tf_op jit(solution)/shard_map/while/body/eval_jaxpr/bpk,ks->bps/dot_general | solution.py:63
  71.6 88.0 %all-gather.3.cloned.1.call-done = f32[64,1,512,128]{3,2,1,0:T(8,128)} async-done(((f32[8,1,512,128]{3,2,1,0:T(8,128)}), f32[64,1,512,128]{3,2,1,0:T(8,128)}) %all-gather.3.cloned.1.call-update) | async-done | bytes 16777232 | tf_op jit(solution)/shard_map/all_gather | solution.py:12
  159.7 8.3 %bitcast_reduce_fusion = f32[8,512,128]{2,1,0:T(8,128)} fusion(f32[8,8,512,128]{3,2,1,0:T(8,128)} %bitcast.119), kind=kLoop, calls=%fused_computation.64 | loop fusion | flops 3670016 | bytes 18874368 | tf_op jit(solution)/shard_map/reduce_sum | solution.py:12
  170.1 88.7 %while.27 = (s32[]{:T(128)}, f32[8,1,8,4096]{3,2,1,0:T(8,128)}, f32[8,1,8,512]{3,2,1,0:T(8,128)}, bf16[8,1,8,512]{3,2,1,0:T(8,128)(2,1)}, bf16[8,1,512,128]{3,2,...) while((s32[]{:T(128)}, f32[8,1,8,4096]{3,2,1,0:T(8,128)}, ...), condition=%wide.region_4.5_spmd.clone, body=%wide.region_3.4_spmd.clone.sunk | while | flops 1200193536 | bytes 30742168 | solution.py:107
  193.6 2.6 fusion.100
  211.8 2.6 fusion.102
  226.8 2.6 fusion.100
  237.9 2.6 fusion.100
  258.8 2.8 copy.18
  261.7 3.1 bitcast_bitcast_fusion
  264.7 2.7 reshape.171
  267.4 10.7 %all_to_all.33 = f32[4,1,8192]{2,1,0:T(1,128)S(1)} all-to-all(f32[4,1,8192]{2,1,0:T(1,128)S(1)} %reshape.171), channel_id=1, replica_groups=mesh['path'=4,'trade'=8] {'path'}, dimensions={0} | all-to-all | bytes 262144 | tf_op jit(solution)/shard_map/all_to_all | solution.py:113
  282.1 2.8 copy.19
  287.2 29.7 %reduce-scatter.2.cloned.1.call-done = f32[4,8,128]{2,1,0:T(8,128)} async-done(((f32[32,8,128]{2,1,0:T(8,128)}), f32[4,8,128]{2,1,0:T(8,128)}) %reduce-scatter.2.cloned.1.call-update) | async-done | bytes 16400 | tf_op jit(solution)/shard_map/reduce_scatter | solution.py:114
  (164 shorter events, 112.7 us)
Async XLA Ops:
  7.2 6.5 %copy-start = (bf16[32,8,4096]{2,1,0:T(8,128)(2,1)S(1)}, bf16[32,8,4096]{2,1,0:T(8,128)(2,1)}, u32[]{:S(2)}) copy-start(bf16[32,8,4096]{2,1,0:T(8,128)(2,1)} %param.14) | copy-start | bytes 6291460
  7.2 12.2 %all-to-all-start = ((bf16[32,8,128]{2,1,0:T(8,128)(2,1)}), bf16[32,8,128]{2,1,0:T(8,128)(2,1)S(1)}, u32[]{:S(2)}, u32[]{:S(2)}) async-start(bf16[32,8,128]{2,1,0:T(8,128)(2,1)} %param.13), calls=%async_computation | async-start | bytes 131072 | tf_op jit(solution)/shard_map/all_to_all | solution.py:35
  13.7 146.0 %all-gather.3.cloned.1.call-start = ((), (), s32[]{:S(2)}) async-start(), calls=%async_computation.4 | async-start | bytes 18874368 | tf_op jit(solution)/shard_map/all_gather | solution.py:12
  19.4 52.0 %copy-start.9 = (f32[32]{0:T(128)S(1)}, f32[32]{0:T(128)}, u32[]{:S(2)}) copy-start(f32[32]{0:T(128)} %param.17) | copy-start | bytes 388
  19.4 52.1 %copy-start.7 = (f32[128]{0:T(128)S(1)}, f32[128]{0:T(128)}, u32[]{:S(2)}) copy-start(f32[128]{0:T(128)} %param.18) | copy-start | bytes 1540
  19.5 5.3 %copy-start.4 = (s32[128]{0:T(128)S(1)}, s32[128]{0:T(128)}, u32[]{:S(2)}) copy-start(s32[128]{0:T(128)} %get-tuple-element.393) | copy-start | bytes 1540 | tf_op jit(solution)/shard_map/while
  25.9 5.3 %copy-start.4 = (s32[128]{0:T(128)S(1)}, s32[128]{0:T(128)}, u32[]{:S(2)}) copy-start(s32[128]{0:T(128)} %get-tuple-element.393) | copy-start | bytes 1540 | tf_op jit(solution)/shard_map/while
  32.4 5.3 %copy-start.4 = (s32[128]{0:T(128)S(1)}, s32[128]{0:T(128)}, u32[]{:S(2)}) copy-start(s32[128]{0:T(128)} %get-tuple-element.393) | copy-start | bytes 1540 | tf_op jit(solution)/shard_map/while
  38.9 5.3 %copy-start.4 = (s32[128]{0:T(128)S(1)}, s32[128]{0:T(128)}, u32[]{:S(2)}) copy-start(s32[128]{0:T(128)} %get-tuple-element.393) | copy-start | bytes 1540 | tf_op jit(solution)/shard_map/while
  45.3 5.3 %copy-start.4 = (s32[128]{0:T(128)S(1)}, s32[128]{0:T(128)}, u32[]{:S(2)}) copy-start(s32[128]{0:T(128)} %get-tuple-element.393) | copy-start | bytes 1540 | tf_op jit(solution)/shard_map/while
  51.8 5.3 %copy-start.4 = (s32[128]{0:T(128)S(1)}, s32[128]{0:T(128)}, u32[]{:S(2)}) copy-start(s32[128]{0:T(128)} %get-tuple-element.393) | copy-start | bytes 1540 | tf_op jit(solution)/shard_map/while
  58.3 5.3 %copy-start.4 = (s32[128]{0:T(128)S(1)}, s32[128]{0:T(128)}, u32[]{:S(2)}) copy-start(s32[128]{0:T(128)} %get-tuple-element.393) | copy-start | bytes 1540 | tf_op jit(solution)/shard_map/while
  64.7 5.3 %copy-start.4 = (s32[128]{0:T(128)S(1)}, s32[128]{0:T(128)}, u32[]{:S(2)}) copy-start(s32[128]{0:T(128)} %get-tuple-element.393) | copy-start | bytes 1540 | tf_op jit(solution)/shard_map/while
  71.2 88.5 %copy-start.1 = (bf16[8,1,8,4096]{3,2,1,0:T(8,128)(2,1)}, bf16[8,1,8,4096]{3,2,1,0:T(8,128)(2,1)S(1)}, u32[]{:S(2)}) copy-start(bf16[8,1,8,4096]{3,2,1,0:T(8,128)(2,1)S(1)} %get-tuple-element.431) | copy-start | bytes 1572868
  71.2 88.5 %copy-start.3 = (bf16[8,1,8,512]{3,2,1,0:T(8,128)(2,1)}, bf16[8,1,8,512]{3,2,1,0:T(8,128)(2,1)S(1)}, u32[]{:S(2)}) copy-start(bf16[8,1,8,512]{3,2,1,0:T(8,128)(2,1)S(1)} %get-tuple-element.438) | copy-start | bytes 196612
  71.2 245.7 %reduce-scatter.2.cloned.1.call-start = ((), (), s32[]{:S(2)}) async-start(), calls=%async_computation.3 | async-start | bytes 147456 | tf_op jit(solution)/shard_map/reduce_scatter | solution.py:114
  159.7 10.4 %copy-start.2 = (f32[4096]{0:T(1024)S(1)}, f32[4096]{0:T(1024)}, u32[]{:S(2)}) copy-start(f32[4096]{0:T(1024)} %get-tuple-element.436) | copy-start | bytes 49156
  159.7 10.4 %copy-start.5 = (s32[128]{0:T(128)S(1)}, s32[128]{0:T(128)}, u32[]{:S(2)}) copy-start(s32[128]{0:T(128)} %get-tuple-element.442) | copy-start | bytes 1540
  198.7 4.7 %copy-start.6 = (s32[128]{0:T(128)S(1)}, s32[128]{0:T(128)}, u32[]{:S(2)}) copy-start(s32[128]{0:T(128)} %get-tuple-element.454) | copy-start | bytes 1540 | tf_op jit(solution)/shard_map/while
  209.8 4.7 %copy-start.6 = (s32[128]{0:T(128)S(1)}, s32[128]{0:T(128)}, u32[]{:S(2)}) copy-start(s32[128]{0:T(128)} %get-tuple-element.454) | copy-start | bytes 1540 | tf_op jit(solution)/shard_map/while
  220.9 4.7 %copy-start.6 = (s32[128]{0:T(128)S(1)}, s32[128]{0:T(128)}, u32[]{:S(2)}) copy-start(s32[128]{0:T(128)} %get-tuple-element.454) | copy-start | bytes 1540 | tf_op jit(solution)/shard_map/while
  232.0 4.7 %copy-start.6 = (s32[128]{0:T(128)S(1)}, s32[128]{0:T(128)}, u32[]{:S(2)}) copy-start(s32[128]{0:T(128)} %get-tuple-element.454) | copy-start | bytes 1540 | tf_op jit(solution)/shard_map/while
  243.1 4.7 %copy-start.6 = (s32[128]{0:T(128)S(1)}, s32[128]{0:T(128)}, u32[]{:S(2)}) copy-start(s32[128]{0:T(128)} %get-tuple-element.454) | copy-start | bytes 1540 | tf_op jit(solution)/shard_map/while
  254.1 4.7 %copy-start.6 = (s32[128]{0:T(128)S(1)}, s32[128]{0:T(128)}, u32[]{:S(2)}) copy-start(s32[128]{0:T(128)} %get-tuple-element.454) | copy-start | bytes 1540 | tf_op jit(solution)/shard_map/while
  (10 other events, 41.0 us)
Sparse Core Ops, SparseCore 0:
  71.3 88.2 all-gather.2
  285.1 31.8 reduce-scatter.1
